TPU v7x, 256 devices: a whole 4x4x8 slice. The times are simulated.
256 devices in a mesh: space: 128 (over y, z, x), mp: 2 (over core).
Axes of the slice: x: 4, y: 4, z: 8, core: 2. Of those that a mesh axis runs over, the one named last changes fastest.
Arguments:
- points: bfloat16 [262144, 512], P('space'), may hold values from -40 to 40
- curve_rank: int32 [262144], P('space'), may hold values from 0 to 262143, as said below
- patch_counts: int32 [128, 4], P('space'), may hold values from 1 to 1024, 2048 in all within a row
- norm_gain_attn: float32 [512], replicated, may hold values from 0.1 to 1.9
- w_qkv: bfloat16 [3, 512, 512], P(None, None, 'mp'), may hold values from -1.5 to 1.5
- w_out: bfloat16 [512, 512], P('mp'), may hold values from -0.75 to 0.75
- norm_gain_mlp: float32 [512], replicated, may hold values from 0.1 to 1.9
- w_fc1: bfloat16 [512, 2048], P(None, 'mp'), may hold values from -0.25 to 0.25
- w_fc2: bfloat16 [2048, 512], P('mp'), may hold values from -0.1875 to 0.1875
Outputs:
- layer_out: bfloat16 [262144, 512], P('space')
Inputs may be any that keep to these rules, and one draw needn't show every extreme that they name: curve_rank is a permutation; the points of shard a take exactly the positions b * 2048 + a * 16 + m for every owner b and every m below 16. `patch_counts`: each row sums to 2048.
All inputs are finite; a program needn't handle non-finite values.
Results may differ from a plain program's by a relative error of at most 0.0075.
Values may be sent and summed in bfloat16 or wider, within the bound.
A program may use at most 128 MiB of HBM per device.

v0:
```python
import math
import jax
import jax.numpy as jnp
from jax import lax
from jax.sharding import PartitionSpec as P

PATCH = 1024
HDIM = 64
epsilon = 1e-06


def layer_norm(inputs, gain_row):
    values = inputs.astype(jnp.float32)
    average = jnp.mean(values, axis=-1, keepdims=True)
    centred = values - average
    second = jnp.mean(centred * centred, axis=-1, keepdims=True)
    return (centred * lax.rsqrt(second + epsilon) * gain_row).astype(jnp.bfloat16)


def tile_layout(counts, tile_width):
    starts = jnp.cumsum(counts) - counts
    offsets = jnp.arange(tile_width, dtype=jnp.int32)
    usable = offsets[None, :] < counts[:, None]
    source = jnp.where(usable, starts[:, None] + offsets[None, :], 0)
    return (starts, source, usable)


def back_index(starts, length, tile_width):
    places = jnp.arange(length, dtype=jnp.int32)
    covered = starts[None, :] <= places[:, None]
    owning = jnp.sum(covered.astype(jnp.int32), axis=1) - 1
    start_of = jnp.max(jnp.where(covered, starts[None, :], 0), axis=1)
    return owning * tile_width + places - start_of


def attend(queries, key_rows, value_rows, counts):
    length, columns = queries.shape
    head_count = columns // HDIM
    score_scale = 1.0 / math.sqrt(HDIM)
    starts, source, usable = tile_layout(counts, PATCH)

    def one_tile(packed):
        picked, allowed = packed
        tile_q = queries[picked].reshape(PATCH, head_count, HDIM)
        tile_k = key_rows[picked].reshape(PATCH, head_count, HDIM)
        tile_v = value_rows[picked].reshape(PATCH, head_count, HDIM)
        scores = (
            jnp.einsum("qhd,khd->hqk", tile_q, tile_k, preferred_element_type=jnp.float32)
            * score_scale
        )
        scores = jnp.where(allowed[None, None, :], scores, -jnp.inf)
        highest = jnp.max(scores, axis=2, keepdims=True)
        raised = jnp.exp(scores - highest)
        weights = (raised / jnp.sum(raised, axis=2, keepdims=True)).astype(jnp.bfloat16)
        context = jnp.einsum("hqk,khd->qhd", weights, tile_v, preferred_element_type=jnp.float32)
        return context.astype(jnp.bfloat16).reshape(PATCH, columns)

    tile_out = lax.map(one_tile, (source, usable))
    places = back_index(starts, length, PATCH)
    return tile_out.reshape(-1, columns)[places]


def project(arrived, w_qkv):
    queries = jnp.dot(arrived, w_qkv[0], preferred_element_type=jnp.float32).astype(jnp.bfloat16)
    key_rows = jnp.dot(arrived, w_qkv[1], preferred_element_type=jnp.float32).astype(jnp.bfloat16)
    value_rows = jnp.dot(arrived, w_qkv[2], preferred_element_type=jnp.float32).astype(jnp.bfloat16)
    return (queries, key_rows, value_rows)


def body(
    points, curve_rank, patch_counts, norm_gain_attn, w_qkv, w_out, norm_gain_mlp, w_fc1, w_fc2
):
    shards = lax.axis_size("space")
    length, features = points.shape
    cell_rows = length // shards
    half_cols = w_qkv.shape[2]
    own_index = lax.axis_index("space")
    owner_id = curve_rank // length
    within = curve_rank % length - own_index * cell_rows
    slot_of = owner_id * cell_rows + within
    senders = jnp.zeros((length,), jnp.int32).at[slot_of].set(jnp.arange(length, dtype=jnp.int32))
    normed = layer_norm(points, norm_gain_attn)
    ordered_send = normed[senders].reshape(shards, cell_rows, features)
    arrived = lax.all_to_all(
        ordered_send, "space", split_axis=0, concat_axis=0, tiled=True
    ).reshape(length, features)
    queries, key_rows, value_rows = project(arrived, w_qkv)
    context = attend(queries, key_rows, value_rows, patch_counts[0])
    chip_size = lax.axis_size("mp")
    half_rows = length // chip_size
    chip_index = lax.axis_index("mp")
    partial_value = jnp.dot(context, w_out, preferred_element_type=jnp.float32)
    summed = lax.psum_scatter(partial_value, "mp", scatter_dimension=1, tiled=True).astype(
        jnp.bfloat16
    )
    returned = lax.all_to_all(
        summed.reshape(shards, cell_rows, half_cols),
        "space",
        split_axis=0,
        concat_axis=0,
        tiled=True,
    )
    returned = returned.reshape(length, half_cols)[slot_of]
    attn_out = lax.all_gather(returned, "mp", axis=1, tiled=True)
    middle = (points.astype(jnp.float32) + attn_out.astype(jnp.float32)).astype(jnp.bfloat16)
    normed_mlp = layer_norm(middle, norm_gain_mlp)
    hidden = jax.nn.gelu(
        jnp.dot(normed_mlp, w_fc1, preferred_element_type=jnp.float32), approximate=True
    ).astype(jnp.bfloat16)
    summed_mlp = lax.psum_scatter(
        jnp.dot(hidden, w_fc2, preferred_element_type=jnp.float32).astype(jnp.bfloat16),
        "mp",
        scatter_dimension=0,
        tiled=True,
    ).astype(jnp.float32)
    middle_rows = lax.dynamic_slice_in_dim(middle, chip_index * half_rows, half_rows, 0)
    finished = (middle_rows.astype(jnp.float32) + summed_mlp).astype(jnp.bfloat16)
    return lax.all_gather(finished, "mp", axis=0, tiled=True)


def solution(mesh):
    placed = (
        P("space", None),
        P("space"),
        P("space", None),
        P(),
        P(None, None, "mp"),
        P("mp", None),
        P(),
        P(None, "mp"),
        P("mp", None),
    )
    return jax.shard_map(
        body, mesh=mesh, in_specs=placed, out_specs=P("space", None), check_vma=False
    )
```

profile of v0, /device:TPU:1, one launch (start us, length us, event | category | flops | bytes accessed | tf_op | source)
XLA Modules:
  0.0 431.5 jit_solution(8900344260000890417)
XLA Ops:
  6.5 2.0 convert_reduce_fusion
  8.6 2.5 fusion.23
  11.7 8.0 %scatter_custom_fusion = s32[2048]{0:T(1024)S(1)} fusion(s32[2048]{0:T(1024)S(1)} %get-tuple-element.62, s32[2048]{0:T(1024)S(1)} %iota.14, s32[]{:T(128)} %constant.44.clone.1), kind=kCustom, calls=%fused_computation.92 | custom fusion | bytes 8196 | tf_op jit(solution)/shard_map/scatter | solution.py:81
  19.8 2.1 fusion.25
  21.9 9.2 %gather_fusion.3 = bf16[2048,512]{1,0:T(8,128)(2,1)} fusion(bf16[2048,512]{1,0:T(8,128)(2,1)S(1)} %fusion.25, s32[2048]{0:T(1024)S(1)} %fusion.54), kind=kCustom, calls=%fused_computation.3 | custom fusion | bytes 4202496 | tf_op jit(solution)/shard_map/gather | solution.py:83
  31.1 16.5 %all-to-all-start = ((bf16[128,16,512]{2,1,0:T(8,128)(2,1)}), bf16[128,16,512]{2,1,0:T(8,128)(2,1)S(1)}, u32[]{:S(2)}, u32[]{:S(2)}) async-start(bf16[128,16,512]{2,1,0:T(8,128)(2,1)} %bitcast.73), calls=%async_computation | async-start | bytes 4194304 | tf_op jit(solution)/shard_map/all_to_all | solution.py:84
  48.9 48.0 %all-to-all-done = bf16[128,16,512]{2,1,0:T(8,128)(2,1)S(1)} async-done(((bf16[128,16,512]{2,1,0:T(8,128)(2,1)}), bf16[128,16,512]{2,1,0:T(8,128)(2,1)S(1)}, u32[]{:S(2)}, u32[]{:S(2)}) %all-to-all-start) | async-done | bytes 2097184 | tf_op jit(solution)/shard_map/all_to_all | solution.py:84
  96.9 1.3 copy-done.1
  98.2 2.4 convolution_convert_fusion
  101.5 1.7 convolution_convert_fusion.2
  103.2 178.8 %while.10 = (s32[]{:T(128)}, bf16[4,1024,256]{2,1,0:T(8,128)(2,1)}, s32[4,1024]{1,0:T(4,128)S(1)}, bf16[2048,256]{1,0:T(8,128)(2,1)}, pred[4,1024]{1,0:T(4,128)(...) while((s32[]{:T(128)}, bf16[4,1024,256]{2,1,0:T(8,128)(2,1)}, ...), condition=%wide.region_7.8_spmd, body=%wide.region_4.7_spmd.sunk | while | flops 1099174912 | bytes 44105308 | solution.py:58
  103.2 4.9 %gather_fusion.1 = bf16[1024,256]{1,0:T(8,128)(2,1)} fusion(bf16[2048,256]{1,0:T(8,128)(2,1)S(1)} %get-tuple-element.133, s32[1024]{0:T(1024)S(1)} %broadcast_clamp_fusion.4), kind=kCustom, calls=%fused_computation.1.clone.1 | custom fusion | bytes 1052672 | tf_op jit(solution)/shard_map/while/body/eval_jaxpr/gather | solution.py:44
  108.2 2.1 copy.33
  110.2 4.9 %gather_fusion.2 = bf16[1024,256]{1,0:T(8,128)(2,1)} fusion(bf16[2048,256]{1,0:T(8,128)(2,1)S(1)} %get-tuple-element.134, s32[1024]{0:T(1024)S(1)} %broadcast_clamp_fusion.4), kind=kCustom, calls=%fused_computation.2.clone.1 | custom fusion | bytes 1052672 | tf_op jit(solution)/shard_map/while/body/eval_jaxpr/gather | solution.py:45
  115.2 2.1 copy.34
  117.3 10.3 %fusion.89 = (f32[4,1024]{1,0:T(4,128)S(1)}, f32[4,1024,1024]{1,2,0:T(8,128)}) fusion(pred[1024]{0:T(1024)(128)(4,1)S(1)} %dynamic-slice_reduce_fusion.2, bf16[1024,4,64]{0,2,1:T(8,128)(2,1)} %bitcast.69, bf16[1024,4,64]{0,2,1:T(8,128)(2,1)} %bitcast.70), kind=kOutput, calls=%fused_computation.103.clone.1 | convolution fusion | flops 553649152 | bytes 17843200 | tf_op jit(solution)/shard_map/while/body/eval_jaxpr/sub | solution.py:53
  127.6 5.9 %gather_fusion = bf16[1024,256]{1,0:T(8,128)(2,1)} fusion(bf16[2048,256]{1,0:T(8,128)(2,1)} %get-tuple-element.131, s32[1024]{0:T(1024)S(1)} %broadcast_clamp_fusion.4), kind=kCustom, calls=%fused_computation.clone.1 | custom fusion | bytes 1052672 | tf_op jit(solution)/shard_map/while/body/eval_jaxpr/gather | solution.py:46
  133.5 2.1 copy.32
  135.6 8.4 %fusion.90 = bf16[4,64,1024]{2,1,0:T(8,128)(2,1)} fusion(bf16[1024,4,64]{0,2,1:T(8,128)(2,1)} %bitcast.71, f32[4,1024,1024]{1,2,0:T(8,128)} %get-tuple-element.110, f32[4,1024]{1,0:T(4,128)S(1)} %get-tuple-element.111), kind=kOutput, calls=%fused_computation.17.clone.1 | convolution fusion | flops 545521664 | bytes 17842176 | tf_op jit(solution)/shard_map/while/body/eval_jaxpr/hqk,khd->qhd/dot_general | solution.py:55
  144.0 2.1 copy.35
  146.0 1.9 constant_dynamic-update-slice_fusion.2
  147.9 4.9 %gather_fusion.1 = bf16[1024,256]{1,0:T(8,128)(2,1)} fusion(bf16[2048,256]{1,0:T(8,128)(2,1)S(1)} %get-tuple-element.133, s32[1024]{0:T(1024)S(1)} %broadcast_clamp_fusion.4), kind=kCustom, calls=%fused_computation.1.clone.1 | custom fusion | bytes 1052672 | tf_op jit(solution)/shard_map/while/body/eval_jaxpr/gather | solution.py:44
  152.9 2.1 copy.33
  154.9 4.9 %gather_fusion.2 = bf16[1024,256]{1,0:T(8,128)(2,1)} fusion(bf16[2048,256]{1,0:T(8,128)(2,1)S(1)} %get-tuple-element.134, s32[1024]{0:T(1024)S(1)} %broadcast_clamp_fusion.4), kind=kCustom, calls=%fused_computation.2.clone.1 | custom fusion | bytes 1052672 | tf_op jit(solution)/shard_map/while/body/eval_jaxpr/gather | solution.py:45
  159.9 2.1 copy.34
  162.0 10.3 %fusion.89 = (f32[4,1024]{1,0:T(4,128)S(1)}, f32[4,1024,1024]{1,2,0:T(8,128)}) fusion(pred[1024]{0:T(1024)(128)(4,1)S(1)} %dynamic-slice_reduce_fusion.2, bf16[1024,4,64]{0,2,1:T(8,128)(2,1)} %bitcast.69, bf16[1024,4,64]{0,2,1:T(8,128)(2,1)} %bitcast.70), kind=kOutput, calls=%fused_computation.103.clone.1 | convolution fusion | flops 553649152 | bytes 17843200 | tf_op jit(solution)/shard_map/while/body/eval_jaxpr/sub | solution.py:53
  172.3 5.9 %gather_fusion = bf16[1024,256]{1,0:T(8,128)(2,1)} fusion(bf16[2048,256]{1,0:T(8,128)(2,1)} %get-tuple-element.131, s32[1024]{0:T(1024)S(1)} %broadcast_clamp_fusion.4), kind=kCustom, calls=%fused_computation.clone.1 | custom fusion | bytes 1052672 | tf_op jit(solution)/shard_map/while/body/eval_jaxpr/gather | solution.py:46
  178.2 2.1 copy.32
  180.3 8.4 %fusion.90 = bf16[4,64,1024]{2,1,0:T(8,128)(2,1)} fusion(bf16[1024,4,64]{0,2,1:T(8,128)(2,1)} %bitcast.71, f32[4,1024,1024]{1,2,0:T(8,128)} %get-tuple-element.110, f32[4,1024]{1,0:T(4,128)S(1)} %get-tuple-element.111), kind=kOutput, calls=%fused_computation.17.clone.1 | convolution fusion | flops 545521664 | bytes 17842176 | tf_op jit(solution)/shard_map/while/body/eval_jaxpr/hqk,khd->qhd/dot_general | solution.py:55
  188.7 2.1 copy.35
  190.7 1.9 constant_dynamic-update-slice_fusion.2
  192.6 4.9 %gather_fusion.1 = bf16[1024,256]{1,0:T(8,128)(2,1)} fusion(bf16[2048,256]{1,0:T(8,128)(2,1)S(1)} %get-tuple-element.133, s32[1024]{0:T(1024)S(1)} %broadcast_clamp_fusion.4), kind=kCustom, calls=%fused_computation.1.clone.1 | custom fusion | bytes 1052672 | tf_op jit(solution)/shard_map/while/body/eval_jaxpr/gather | solution.py:44
  197.6 2.1 copy.33
  199.6 4.9 %gather_fusion.2 = bf16[1024,256]{1,0:T(8,128)(2,1)} fusion(bf16[2048,256]{1,0:T(8,128)(2,1)S(1)} %get-tuple-element.134, s32[1024]{0:T(1024)S(1)} %broadcast_clamp_fusion.4), kind=kCustom, calls=%fused_computation.2.clone.1 | custom fusion | bytes 1052672 | tf_op jit(solution)/shard_map/while/body/eval_jaxpr/gather | solution.py:45
  204.6 2.1 copy.34
  206.7 10.3 %fusion.89 = (f32[4,1024]{1,0:T(4,128)S(1)}, f32[4,1024,1024]{1,2,0:T(8,128)}) fusion(pred[1024]{0:T(1024)(128)(4,1)S(1)} %dynamic-slice_reduce_fusion.2, bf16[1024,4,64]{0,2,1:T(8,128)(2,1)} %bitcast.69, bf16[1024,4,64]{0,2,1:T(8,128)(2,1)} %bitcast.70), kind=kOutput, calls=%fused_computation.103.clone.1 | convolution fusion | flops 553649152 | bytes 17843200 | tf_op jit(solution)/shard_map/while/body/eval_jaxpr/sub | solution.py:53
  217.0 5.9 %gather_fusion = bf16[1024,256]{1,0:T(8,128)(2,1)} fusion(bf16[2048,256]{1,0:T(8,128)(2,1)} %get-tuple-element.131, s32[1024]{0:T(1024)S(1)} %broadcast_clamp_fusion.4), kind=kCustom, calls=%fused_computation.clone.1 | custom fusion | bytes 1052672 | tf_op jit(solution)/shard_map/while/body/eval_jaxpr/gather | solution.py:46
  222.9 2.1 copy.32
  225.0 8.4 %fusion.90 = bf16[4,64,1024]{2,1,0:T(8,128)(2,1)} fusion(bf16[1024,4,64]{0,2,1:T(8,128)(2,1)} %bitcast.71, f32[4,1024,1024]{1,2,0:T(8,128)} %get-tuple-element.110, f32[4,1024]{1,0:T(4,128)S(1)} %get-tuple-element.111), kind=kOutput, calls=%fused_computation.17.clone.1 | convolution fusion | flops 545521664 | bytes 17842176 | tf_op jit(solution)/shard_map/while/body/eval_jaxpr/hqk,khd->qhd/dot_general | solution.py:55
  233.4 2.1 copy.35
  235.4 1.9 constant_dynamic-update-slice_fusion.2
  237.3 4.9 %gather_fusion.1 = bf16[1024,256]{1,0:T(8,128)(2,1)} fusion(bf16[2048,256]{1,0:T(8,128)(2,1)S(1)} %get-tuple-element.133, s32[1024]{0:T(1024)S(1)} %broadcast_clamp_fusion.4), kind=kCustom, calls=%fused_computation.1.clone.1 | custom fusion | bytes 1052672 | tf_op jit(solution)/shard_map/while/body/eval_jaxpr/gather | solution.py:44
  242.3 2.1 copy.33
  244.3 4.9 %gather_fusion.2 = bf16[1024,256]{1,0:T(8,128)(2,1)} fusion(bf16[2048,256]{1,0:T(8,128)(2,1)S(1)} %get-tuple-element.134, s32[1024]{0:T(1024)S(1)} %broadcast_clamp_fusion.4), kind=kCustom, calls=%fused_computation.2.clone.1 | custom fusion | bytes 1052672 | tf_op jit(solution)/shard_map/while/body/eval_jaxpr/gather | solution.py:45
  249.3 2.1 copy.34
  251.4 10.3 %fusion.89 = (f32[4,1024]{1,0:T(4,128)S(1)}, f32[4,1024,1024]{1,2,0:T(8,128)}) fusion(pred[1024]{0:T(1024)(128)(4,1)S(1)} %dynamic-slice_reduce_fusion.2, bf16[1024,4,64]{0,2,1:T(8,128)(2,1)} %bitcast.69, bf16[1024,4,64]{0,2,1:T(8,128)(2,1)} %bitcast.70), kind=kOutput, calls=%fused_computation.103.clone.1 | convolution fusion | flops 553649152 | bytes 17843200 | tf_op jit(solution)/shard_map/while/body/eval_jaxpr/sub | solution.py:53
  261.7 5.9 %gather_fusion = bf16[1024,256]{1,0:T(8,128)(2,1)} fusion(bf16[2048,256]{1,0:T(8,128)(2,1)} %get-tuple-element.131, s32[1024]{0:T(1024)S(1)} %broadcast_clamp_fusion.4), kind=kCustom, calls=%fused_computation.clone.1 | custom fusion | bytes 1052672 | tf_op jit(solution)/shard_map/while/body/eval_jaxpr/gather | solution.py:46
  267.6 2.1 copy.32
  269.7 8.4 %fusion.90 = bf16[4,64,1024]{2,1,0:T(8,128)(2,1)} fusion(bf16[1024,4,64]{0,2,1:T(8,128)(2,1)} %bitcast.71, f32[4,1024,1024]{1,2,0:T(8,128)} %get-tuple-element.110, f32[4,1024]{1,0:T(4,128)S(1)} %get-tuple-element.111), kind=kOutput, calls=%fused_computation.17.clone.1 | convolution fusion | flops 545521664 | bytes 17842176 | tf_op jit(solution)/shard_map/while/body/eval_jaxpr/hqk,khd->qhd/dot_general | solution.py:55
  278.1 2.1 copy.35
  280.1 1.9 constant_dynamic-update-slice_fusion.2
  282.0 8.5 %gather_fusion.4 = bf16[2048,256]{1,0:T(8,128)(2,1)S(1)} fusion(bf16[4096,256]{1,0:T(8,128)(2,1)} %bitcast.68, s32[2048]{0:T(1024)S(1)} %copy-done.5), kind=kCustom, calls=%fused_computation.4 | custom fusion | bytes 2105344 | tf_op jit(solution)/shard_map/gather | solution.py:60
  290.6 2.6 fusion.68
  293.3 15.8 %reduce-scatter.3.cloned.1.call-done = f32[2048,256]{1,0:T(8,128)} async-done(((f32[2048,512]{1,0:T(8,128)}), f32[2048,256]{1,0:T(8,128)}) %reduce-scatter.3.cloned.1.call-update) | async-done | bytes 2097168 | tf_op jit(solution)/shard_map/reduce_scatter | solution.py:93
  309.1 1.7 convert_element_type.64
  310.8 40.7 %all_to_all.10 = bf16[128,16,256]{2,1,0:T(8,128)(2,1)S(1)} all-to-all(bf16[128,16,256]{2,1,0:T(8,128)(2,1)S(1)} %bitcast.74), channel_id=1, replica_groups=mesh['space'=128,'mp'=2] {'space'}, dimensions={0} | all-to-all | bytes 2097152 | tf_op jit(solution)/shard_map/all_to_all | solution.py:96
  351.5 9.1 %gather_fusion.5 = bf16[2048,256]{1,0:T(8,128)(2,1)} fusion(bf16[2048,256]{1,0:T(8,128)(2,1)S(1)} %bitcast.67, s32[2048]{0:T(1024)S(1)} %copy-done.4), kind=kCustom, calls=%fused_computation.5 | custom fusion | bytes 2105344 | tf_op jit(solution)/shard_map/gather | solution.py:103
  360.9 13.2 %all-gather.6.cloned.1.call-done = bf16[2048,512]{1,0:T(8,128)(2,1)} async-done(((bf16[2048,256]{1,0:T(8,128)(2,1)}), bf16[2048,512]{1,0:T(8,128)(2,1)}) %all-gather.6.cloned.1.call-update) | async-done | bytes 2097168 | tf_op jit(solution)/shard_map/all_gather | solution.py:104
  374.1 2.9 convert_reduce_fusion.1
  378.1 7.3 %fusion.32 = bf16[2048,512]{1,0:T(8,128)(2,1)} fusion(bf16[1024,512]{1,0:T(8,128)(2,1)S(1)} %copy-done, bf16[512,1024]{1,0:T(8,128)(2,1)} %param.18, bf16[2048,512]{1,0:T(8,128)(2,1)S(1)} %get-tuple-element.60, f32[512]{0:T(512)S(1)} %copy-done.10, f32[2048]{0:T(1024)S(1)} %add_rsqrt_fusion, f32[2048]{0:T(1024)S(1)} %broadcast_multiply_fusion), kind=kOutput, calls=%fused_computation.50 | convolution fusion | flops 4320133120 | bytes 6309888 | tf_op jit(solution)/shard_map/dot_general | solution.py:111
  385.5 16.1 %reduce-scatter.5.cloned.1.call-done = bf16[1024,512]{1,0:T(8,128)(2,1)} async-done(((bf16[2048,512]{1,0:T(8,128)(2,1)}), bf16[1024,512]{1,0:T(8,128)(2,1)}) %reduce-scatter.5.cloned.1.call-update) | async-done | bytes 1048592 | tf_op jit(solution)/shard_map/reduce_scatter | solution.py:110
  401.5 2.5 add_convert_fusion
  404.0 17.9 %all-gather.4.cloned.1.call-done = bf16[2048,512]{1,0:T(8,128)(2,1)} async-done(((bf16[1024,512]{1,0:T(8,128)(2,1)}), bf16[2048,512]{1,0:T(8,128)(2,1)}) %all-gather.4.cloned.1.call-update) | async-done | bytes 2097168 | tf_op jit(solution)/shard_map/all_gather | solution.py:118
  421.9 3.0 copy.44
  (60 shorter events, 4.4 us)
Async XLA Ops:
  6.5 371.6 %copy-start = (bf16[1024,512]{1,0:T(8,128)(2,1)S(1)}, bf16[1024,512]{1,0:T(8,128)(2,1)}, u32[]{:S(2)}) copy-start(bf16[1024,512]{1,0:T(8,128)(2,1)} %param.19) | copy-start | bytes 3145732
  6.5 4.5 %copy-start.6 = (s32[2048]{0:T(1024)S(1)}, s32[2048]{0:T(1024)}, u32[]{:S(2)}) copy-start(s32[2048]{0:T(1024)} %param.12) | copy-start | bytes 24580
  6.5 13.2 %copy-start.7 = (f32[512]{0:T(512)S(1)}, f32[512]{0:T(512)}, u32[]{:S(2)}) copy-start(f32[512]{0:T(512)} %param.14) | copy-start | bytes 6148
  31.1 16.7 %copy-start.8 = (s32[1,4]{1,0:T(1,128)S(1)}, s32[1,4]{1,0:T(1,128)}, u32[]{:S(2)}) copy-start(s32[1,4]{1,0:T(1,128)} %param.13) | copy-start | bytes 52
  31.1 65.8 %all-to-all-start = ((bf16[128,16,512]{2,1,0:T(8,128)(2,1)}), bf16[128,16,512]{2,1,0:T(8,128)(2,1)S(1)}, u32[]{:S(2)}, u32[]{:S(2)}) async-start(bf16[128,16,512]{2,1,0:T(8,128)(2,1)} %bitcast.73), calls=%async_computation | async-start | bytes 4194304 | tf_op jit(solution)/shard_map/all_to_all | solution.py:84
  47.5 261.6 %reduce-scatter.3.cloned.1.call-start = ((), (), s32[]{:S(2)}) async-start(), calls=%async_computation.4 | async-start | bytes 6291456 | tf_op jit(solution)/shard_map/reduce_scatter | solution.py:93
  96.9 1.4 copy-start.1
  98.2 2.5 copy-start.9
  98.2 2.6 copy-start.2
  103.2 178.8 %copy-start.5 = (s32[2048]{0:T(1024)S(1)}, s32[2048]{0:T(1024)}, u32[]{:S(2)}) copy-start(s32[2048]{0:T(1024)} %broadcast_clamp_fusion.1) | copy-start | bytes 24580
  282.0 8.6 %copy-start.3 = (bf16[256,512]{1,0:T(8,128)(2,1)S(1)}, bf16[256,512]{1,0:T(8,128)(2,1)}, u32[]{:S(2)}) copy-start(bf16[256,512]{1,0:T(8,128)(2,1)} %param.16) | copy-start | bytes 786436
  293.2 58.3 %copy-start.4 = (s32[2048]{0:T(1024)S(1)}, s32[2048]{0:T(1024)}, u32[]{:S(2)}) copy-start(s32[2048]{0:T(1024)} %get-tuple-element.61) | copy-start | bytes 24580
  293.2 80.9 %all-gather.6.cloned.1.call-start = ((), (), s32[]{:S(2)}) async-start(), calls=%async_computation.7 | async-start | bytes 3145728 | tf_op jit(solution)/shard_map/all_gather | solution.py:104
  360.6 17.5 %copy-start.10 = (f32[512]{0:T(512)S(1)}, f32[512]{0:T(512)}, u32[]{:S(2)}) copy-start(f32[512]{0:T(512)} %param.17) | copy-start | bytes 6148
  360.6 40.9 %reduce-scatter.5.cloned.1.call-start = ((), (), s32[]{:S(2)}) async-start(), calls=%async_computation.5 | async-start | bytes 3145728 | tf_op jit(solution)/shard_map/reduce_scatter | solution.py:110
  385.4 36.5 %all-gather.4.cloned.1.call-start = ((), (), s32[]{:S(2)}) async-start(), calls=%async_computation.6 | async-start | bytes 3145728 | tf_op jit(solution)/shard_map/all_gather | solution.py:118
Sparse Core Ops, SparseCore 0:
  293.4 15.7 reduce-scatter.2
  360.7 13.3 all-gather.5
  385.5 15.9 reduce-scatter.4
  404.2 17.7 all-gather.3
where the time goes:
time: 433 us; the launch traced here: 432 us
  local copies, waits for them, and re-layouts  143 us (33%)
  waiting for transfers between devices  111 us (26%)
  matrix products  89.6 us (21%)
  blocking collectives  40.7 us (9%)
  starting transfers between devices  17 us (4%)
  other arithmetic  16.5 us (4%)
  between operations  13.3 us (3%)
    all_to_all x1, waiting for transfers between devices, body(): lax.all_to_all(ordered_send, 'space', split_axis=0, concat_axis=0, tiled=...  48 us
    sub x4, matrix products, one_tile(): raised = jnp.exp(scores - highest)  41.4 us
    all_to_all x1, blocking collectives, body(): lax.all_to_all(summed.reshape(shards, cell_rows, half_cols), 'space', spl...  40.7 us
    dot_general x4, matrix products, one_tile(): jnp.einsum('hqk,khd->qhd', weights, tile_v, preferred_element_type=jnp.fl...  33.5 us
    gather x8, local copies, waits for them, and re-layouts, one_tile(): tile_v = value_rows[picked].reshape(PATCH, head_count, HDIM)  32 us
    gather x8, local copies, waits for them, and re-layouts, one_tile(): tile_q = queries[picked].reshape(PATCH, head_count, HDIM)  28.1 us
    gather x8, local copies, waits for them, and re-layouts, one_tile(): tile_k = key_rows[picked].reshape(PATCH, head_count, HDIM)  28 us
    all_gather x1, waiting for transfers between devices, body(): return lax.all_gather(finished, 'mp', axis=0, tiled=True)  17.9 us
  transfers between devices with their start and end apart: 5, of which 5 were waited for; matrix products, arithmetic and copies ran while one was open for 0% of the time, Pallas kernels for 0%

commit v1 on v0

--- a/solution.py
+++ b/solution.py
@@ -101,7 +101,8 @@
         tiled=True,
     )
     returned = returned.reshape(length, half_cols)[slot_of]
-    attn_out = lax.all_gather(returned, "mp", axis=1, tiled=True)
+    sent = jnp.stack([returned] * lax.axis_size("mp"))
+    attn_out = jnp.concatenate(lax.all_to_all(sent, "mp", 0, 0), axis=1)
     middle = (points.astype(jnp.float32) + attn_out.astype(jnp.float32)).astype(jnp.bfloat16)
     normed_mlp = layer_norm(middle, norm_gain_mlp)
     hidden = jax.nn.gelu(

time: 433 us -> 420 us (0.970)
  waiting for transfers between devices: 111 us -> 91.4 us
  blocking collectives: 40.7 us -> 49.2 us
    all_gather x1 -> x0, waiting for transfers between devices: 13.2 us -> none  [body(): attn_out = lax.all_gather(returned, 'mp', axis=1, tiled=True)]
    all_to_all x0 -> x1, blocking collectives: none -> 8.47 us  [body(): attn_out = jnp.concatenate(lax.all_to_all(sent, 'mp', 0, 0), axis=1)]
    reduce_scatter x1, waiting for transfers between devices: 16.1 us -> 9.61 us  [body(): lax.psum_scatter(jnp.dot(hidden, w_fc2, preferred_element_type=jnp.float3...]
  transfers between devices with their start and end apart: 5 -> 4, of which waited for: 5 -> 4; matrix products, arithmetic and copies ran while one was open for 0% -> 0% of each run, Pallas kernels for 0% -> 0%
where the time goes in v1:
time: 420 us; the launch traced here: 418 us
  local copies, waits for them, and re-layouts  143 us (34%)
  waiting for transfers between devices  91.4 us (22%)
  matrix products  89.6 us (21%)
  blocking collectives  49.2 us (12%)
  starting transfers between devices  16.8 us (4%)
  other arithmetic  14.6 us (3%)
  between operations  13.4 us (3%)
    all_to_all x1, waiting for transfers between devices, body(): lax.all_to_all(ordered_send, 'space', split_axis=0, concat_axis=0, tiled=...  48 us
    sub x4, matrix products, one_tile(): raised = jnp.exp(scores - highest)  41.4 us
    all_to_all x1, blocking collectives, body(): lax.all_to_all(summed.reshape(shards, cell_rows, half_cols), 'space', spl...  40.7 us
    dot_general x4, matrix products, one_tile(): jnp.einsum('hqk,khd->qhd', weights, tile_v, preferred_element_type=jnp.fl...  33.5 us
    gather x8, local copies, waits for them, and re-layouts, one_tile(): tile_v = value_rows[picked].reshape(PATCH, head_count, HDIM)  32 us
    gather x8, local copies, waits for them, and re-layouts, one_tile(): tile_q = queries[picked].reshape(PATCH, head_count, HDIM)  28.1 us
    gather x8, local copies, waits for them, and re-layouts, one_tile(): tile_k = key_rows[picked].reshape(PATCH, head_count, HDIM)  28 us
    all_gather x1, waiting for transfers between devices, body(): return lax.all_gather(finished, 'mp', axis=0, tiled=True)  17.9 us
  transfers between devices with their start and end apart: 4, of which 4 were waited for; matrix products, arithmetic and copies ran while one was open for 0% of the time, Pallas kernels for 0%

profile of v1, /device:TPU:1, one launch (start us, length us, event | category | flops | bytes accessed | tf_op | source)
XLA Modules:
  0.0 418.2 jit_solution(12342200251017675027)
XLA Ops:
  6.5 2.0 convert_reduce_fusion
  8.6 2.5 fusion.23
  11.7 8.0 %scatter_custom_fusion = s32[2048]{0:T(1024)S(1)} fusion(s32[2048]{0:T(1024)S(1)} %get-tuple-element.62, s32[2048]{0:T(1024)S(1)} %iota.14, s32[]{:T(128)} %constant.44.clone.1), kind=kCustom, calls=%fused_computation.94 | custom fusion | bytes 8196 | tf_op jit(solution)/shard_map/scatter | solution.py:81
  19.8 2.1 fusion.25
  21.9 9.2 %gather_fusion.3 = bf16[2048,512]{1,0:T(8,128)(2,1)} fusion(bf16[2048,512]{1,0:T(8,128)(2,1)S(1)} %fusion.25, s32[2048]{0:T(1024)S(1)} %fusion.54), kind=kCustom, calls=%fused_computation.3 | custom fusion | bytes 4202496 | tf_op jit(solution)/shard_map/gather | solution.py:83
  31.1 16.5 %all-to-all-start = ((bf16[128,16,512]{2,1,0:T(8,128)(2,1)}), bf16[128,16,512]{2,1,0:T(8,128)(2,1)S(1)}, u32[]{:S(2)}, u32[]{:S(2)}) async-start(bf16[128,16,512]{2,1,0:T(8,128)(2,1)} %bitcast.79), calls=%async_computation | async-start | bytes 4194304 | tf_op jit(solution)/shard_map/all_to_all | solution.py:84
  48.9 48.0 %all-to-all-done = bf16[128,16,512]{2,1,0:T(8,128)(2,1)S(1)} async-done(((bf16[128,16,512]{2,1,0:T(8,128)(2,1)}), bf16[128,16,512]{2,1,0:T(8,128)(2,1)S(1)}, u32[]{:S(2)}, u32[]{:S(2)}) %all-to-all-start) | async-done | bytes 2097184 | tf_op jit(solution)/shard_map/all_to_all | solution.py:84
  96.9 1.3 copy-done.2
  98.2 2.4 convolution_convert_fusion
  101.5 1.7 convolution_convert_fusion.2
  103.2 178.8 %while.10 = (s32[]{:T(128)}, bf16[4,1024,256]{2,1,0:T(8,128)(2,1)}, s32[4,1024]{1,0:T(4,128)S(1)}, bf16[2048,256]{1,0:T(8,128)(2,1)}, pred[4,1024]{1,0:T(4,128)(...) while((s32[]{:T(128)}, bf16[4,1024,256]{2,1,0:T(8,128)(2,1)}, ...), condition=%wide.region_7.8_spmd, body=%wide.region_4.7_spmd.sunk | while | flops 1099174912 | bytes 44105308 | solution.py:58
  103.2 4.9 %gather_fusion.1 = bf16[1024,256]{1,0:T(8,128)(2,1)} fusion(bf16[2048,256]{1,0:T(8,128)(2,1)S(1)} %get-tuple-element.133, s32[1024]{0:T(1024)S(1)} %broadcast_clamp_fusion.4), kind=kCustom, calls=%fused_computation.1.clone.1 | custom fusion | bytes 1052672 | tf_op jit(solution)/shard_map/while/body/eval_jaxpr/gather | solution.py:44
  108.2 2.1 copy.37
  110.2 4.9 %gather_fusion.2 = bf16[1024,256]{1,0:T(8,128)(2,1)} fusion(bf16[2048,256]{1,0:T(8,128)(2,1)S(1)} %get-tuple-element.134, s32[1024]{0:T(1024)S(1)} %broadcast_clamp_fusion.4), kind=kCustom, calls=%fused_computation.2.clone.1 | custom fusion | bytes 1052672 | tf_op jit(solution)/shard_map/while/body/eval_jaxpr/gather | solution.py:45
  115.2 2.1 copy.38
  117.3 10.3 %fusion.89 = (f32[4,1024]{1,0:T(4,128)S(1)}, f32[4,1024,1024]{1,2,0:T(8,128)}) fusion(pred[1024]{0:T(1024)(128)(4,1)S(1)} %dynamic-slice_reduce_fusion.2, bf16[1024,4,64]{0,2,1:T(8,128)(2,1)} %bitcast.75, bf16[1024,4,64]{0,2,1:T(8,128)(2,1)} %bitcast.76), kind=kOutput, calls=%fused_computation.105.clone.1 | convolution fusion | flops 553649152 | bytes 17843200 | tf_op jit(solution)/shard_map/while/body/eval_jaxpr/sub | solution.py:53
  127.6 5.9 %gather_fusion = bf16[1024,256]{1,0:T(8,128)(2,1)} fusion(bf16[2048,256]{1,0:T(8,128)(2,1)} %get-tuple-element.131, s32[1024]{0:T(1024)S(1)} %broadcast_clamp_fusion.4), kind=kCustom, calls=%fused_computation.clone.1 | custom fusion | bytes 1052672 | tf_op jit(solution)/shard_map/while/body/eval_jaxpr/gather | solution.py:46
  133.5 2.1 copy.36
  135.6 8.4 %fusion.90 = bf16[4,64,1024]{2,1,0:T(8,128)(2,1)} fusion(bf16[1024,4,64]{0,2,1:T(8,128)(2,1)} %bitcast.77, f32[4,1024,1024]{1,2,0:T(8,128)} %get-tuple-element.110, f32[4,1024]{1,0:T(4,128)S(1)} %get-tuple-element.111), kind=kOutput, calls=%fused_computation.17.clone.1 | convolution fusion | flops 545521664 | bytes 17842176 | tf_op jit(solution)/shard_map/while/body/eval_jaxpr/hqk,khd->qhd/dot_general | solution.py:55
  144.0 2.1 copy.39
  146.0 1.9 constant_dynamic-update-slice_fusion.2
  147.9 4.9 %gather_fusion.1 = bf16[1024,256]{1,0:T(8,128)(2,1)} fusion(bf16[2048,256]{1,0:T(8,128)(2,1)S(1)} %get-tuple-element.133, s32[1024]{0:T(1024)S(1)} %broadcast_clamp_fusion.4), kind=kCustom, calls=%fused_computation.1.clone.1 | custom fusion | bytes 1052672 | tf_op jit(solution)/shard_map/while/body/eval_jaxpr/gather | solution.py:44
  152.9 2.1 copy.37
  154.9 4.9 %gather_fusion.2 = bf16[1024,256]{1,0:T(8,128)(2,1)} fusion(bf16[2048,256]{1,0:T(8,128)(2,1)S(1)} %get-tuple-element.134, s32[1024]{0:T(1024)S(1)} %broadcast_clamp_fusion.4), kind=kCustom, calls=%fused_computation.2.clone.1 | custom fusion | bytes 1052672 | tf_op jit(solution)/shard_map/while/body/eval_jaxpr/gather | solution.py:45
  159.9 2.1 copy.38
  162.0 10.3 %fusion.89 = (f32[4,1024]{1,0:T(4,128)S(1)}, f32[4,1024,1024]{1,2,0:T(8,128)}) fusion(pred[1024]{0:T(1024)(128)(4,1)S(1)} %dynamic-slice_reduce_fusion.2, bf16[1024,4,64]{0,2,1:T(8,128)(2,1)} %bitcast.75, bf16[1024,4,64]{0,2,1:T(8,128)(2,1)} %bitcast.76), kind=kOutput, calls=%fused_computation.105.clone.1 | convolution fusion | flops 553649152 | bytes 17843200 | tf_op jit(solution)/shard_map/while/body/eval_jaxpr/sub | solution.py:53
  172.3 5.9 %gather_fusion = bf16[1024,256]{1,0:T(8,128)(2,1)} fusion(bf16[2048,256]{1,0:T(8,128)(2,1)} %get-tuple-element.131, s32[1024]{0:T(1024)S(1)} %broadcast_clamp_fusion.4), kind=kCustom, calls=%fused_computation.clone.1 | custom fusion | bytes 1052672 | tf_op jit(solution)/shard_map/while/body/eval_jaxpr/gather | solution.py:46
  178.2 2.1 copy.36
  180.3 8.4 %fusion.90 = bf16[4,64,1024]{2,1,0:T(8,128)(2,1)} fusion(bf16[1024,4,64]{0,2,1:T(8,128)(2,1)} %bitcast.77, f32[4,1024,1024]{1,2,0:T(8,128)} %get-tuple-element.110, f32[4,1024]{1,0:T(4,128)S(1)} %get-tuple-element.111), kind=kOutput, calls=%fused_computation.17.clone.1 | convolution fusion | flops 545521664 | bytes 17842176 | tf_op jit(solution)/shard_map/while/body/eval_jaxpr/hqk,khd->qhd/dot_general | solution.py:55
  188.7 2.1 copy.39
  190.7 1.9 constant_dynamic-update-slice_fusion.2
  192.6 4.9 %gather_fusion.1 = bf16[1024,256]{1,0:T(8,128)(2,1)} fusion(bf16[2048,256]{1,0:T(8,128)(2,1)S(1)} %get-tuple-element.133, s32[1024]{0:T(1024)S(1)} %broadcast_clamp_fusion.4), kind=kCustom, calls=%fused_computation.1.clone.1 | custom fusion | bytes 1052672 | tf_op jit(solution)/shard_map/while/body/eval_jaxpr/gather | solution.py:44
  197.6 2.1 copy.37
  199.6 4.9 %gather_fusion.2 = bf16[1024,256]{1,0:T(8,128)(2,1)} fusion(bf16[2048,256]{1,0:T(8,128)(2,1)S(1)} %get-tuple-element.134, s32[1024]{0:T(1024)S(1)} %broadcast_clamp_fusion.4), kind=kCustom, calls=%fused_computation.2.clone.1 | custom fusion | bytes 1052672 | tf_op jit(solution)/shard_map/while/body/eval_jaxpr/gather | solution.py:45
  204.6 2.1 copy.38
  206.7 10.3 %fusion.89 = (f32[4,1024]{1,0:T(4,128)S(1)}, f32[4,1024,1024]{1,2,0:T(8,128)}) fusion(pred[1024]{0:T(1024)(128)(4,1)S(1)} %dynamic-slice_reduce_fusion.2, bf16[1024,4,64]{0,2,1:T(8,128)(2,1)} %bitcast.75, bf16[1024,4,64]{0,2,1:T(8,128)(2,1)} %bitcast.76), kind=kOutput, calls=%fused_computation.105.clone.1 | convolution fusion | flops 553649152 | bytes 17843200 | tf_op jit(solution)/shard_map/while/body/eval_jaxpr/sub | solution.py:53
  217.0 5.9 %gather_fusion = bf16[1024,256]{1,0:T(8,128)(2,1)} fusion(bf16[2048,256]{1,0:T(8,128)(2,1)} %get-tuple-element.131, s32[1024]{0:T(1024)S(1)} %broadcast_clamp_fusion.4), kind=kCustom, calls=%fused_computation.clone.1 | custom fusion | bytes 1052672 | tf_op jit(solution)/shard_map/while/body/eval_jaxpr/gather | solution.py:46
  222.9 2.1 copy.36
  225.0 8.4 %fusion.90 = bf16[4,64,1024]{2,1,0:T(8,128)(2,1)} fusion(bf16[1024,4,64]{0,2,1:T(8,128)(2,1)} %bitcast.77, f32[4,1024,1024]{1,2,0:T(8,128)} %get-tuple-element.110, f32[4,1024]{1,0:T(4,128)S(1)} %get-tuple-element.111), kind=kOutput, calls=%fused_computation.17.clone.1 | convolution fusion | flops 545521664 | bytes 17842176 | tf_op jit(solution)/shard_map/while/body/eval_jaxpr/hqk,khd->qhd/dot_general | solution.py:55
  233.4 2.1 copy.39
  235.4 1.9 constant_dynamic-update-slice_fusion.2
  237.3 4.9 %gather_fusion.1 = bf16[1024,256]{1,0:T(8,128)(2,1)} fusion(bf16[2048,256]{1,0:T(8,128)(2,1)S(1)} %get-tuple-element.133, s32[1024]{0:T(1024)S(1)} %broadcast_clamp_fusion.4), kind=kCustom, calls=%fused_computation.1.clone.1 | custom fusion | bytes 1052672 | tf_op jit(solution)/shard_map/while/body/eval_jaxpr/gather | solution.py:44
  242.3 2.1 copy.37
  244.3 4.9 %gather_fusion.2 = bf16[1024,256]{1,0:T(8,128)(2,1)} fusion(bf16[2048,256]{1,0:T(8,128)(2,1)S(1)} %get-tuple-element.134, s32[1024]{0:T(1024)S(1)} %broadcast_clamp_fusion.4), kind=kCustom, calls=%fused_computation.2.clone.1 | custom fusion | bytes 1052672 | tf_op jit(solution)/shard_map/while/body/eval_jaxpr/gather | solution.py:45
  249.3 2.1 copy.38
  251.4 10.3 %fusion.89 = (f32[4,1024]{1,0:T(4,128)S(1)}, f32[4,1024,1024]{1,2,0:T(8,128)}) fusion(pred[1024]{0:T(1024)(128)(4,1)S(1)} %dynamic-slice_reduce_fusion.2, bf16[1024,4,64]{0,2,1:T(8,128)(2,1)} %bitcast.75, bf16[1024,4,64]{0,2,1:T(8,128)(2,1)} %bitcast.76), kind=kOutput, calls=%fused_computation.105.clone.1 | convolution fusion | flops 553649152 | bytes 17843200 | tf_op jit(solution)/shard_map/while/body/eval_jaxpr/sub | solution.py:53
  261.7 5.9 %gather_fusion = bf16[1024,256]{1,0:T(8,128)(2,1)} fusion(bf16[2048,256]{1,0:T(8,128)(2,1)} %get-tuple-element.131, s32[1024]{0:T(1024)S(1)} %broadcast_clamp_fusion.4), kind=kCustom, calls=%fused_computation.clone.1 | custom fusion | bytes 1052672 | tf_op jit(solution)/shard_map/while/body/eval_jaxpr/gather | solution.py:46
  267.6 2.1 copy.36
  269.7 8.4 %fusion.90 = bf16[4,64,1024]{2,1,0:T(8,128)(2,1)} fusion(bf16[1024,4,64]{0,2,1:T(8,128)(2,1)} %bitcast.77, f32[4,1024,1024]{1,2,0:T(8,128)} %get-tuple-element.110, f32[4,1024]{1,0:T(4,128)S(1)} %get-tuple-element.111), kind=kOutput, calls=%fused_computation.17.clone.1 | convolution fusion | flops 545521664 | bytes 17842176 | tf_op jit(solution)/shard_map/while/body/eval_jaxpr/hqk,khd->qhd/dot_general | solution.py:55
  278.1 2.1 copy.39
  280.1 1.9 constant_dynamic-update-slice_fusion.2
  282.0 8.5 %gather_fusion.4 = bf16[2048,256]{1,0:T(8,128)(2,1)S(1)} fusion(bf16[4096,256]{1,0:T(8,128)(2,1)} %bitcast.73, s32[2048]{0:T(1024)S(1)} %copy-done.6), kind=kCustom, calls=%fused_computation.4 | custom fusion | bytes 2105344 | tf_op jit(solution)/shard_map/gather | solution.py:60
  290.6 2.6 fusion.68
  293.3 15.8 %reduce-scatter.3.cloned.1.call-done = f32[2048,256]{1,0:T(8,128)} async-done(((f32[2048,512]{1,0:T(8,128)}), f32[2048,256]{1,0:T(8,128)}) %reduce-scatter.3.cloned.1.call-update) | async-done | bytes 2097168 | tf_op jit(solution)/shard_map/reduce_scatter | solution.py:93
  309.1 1.7 convert_element_type.70
  310.8 40.7 %all_to_all.15 = bf16[128,16,256]{2,1,0:T(8,128)(2,1)S(1)} all-to-all(bf16[128,16,256]{2,1,0:T(8,128)(2,1)S(1)} %bitcast.80), channel_id=1, replica_groups=mesh['space'=128,'mp'=2] {'space'}, dimensions={0} | all-to-all | bytes 2097152 | tf_op jit(solution)/shard_map/all_to_all | solution.py:96
  351.5 7.5 %gather_fusion.5 = bf16[2048,256]{1,0:T(8,128)(2,1)S(1)} fusion(bf16[2048,256]{1,0:T(8,128)(2,1)S(1)} %bitcast.72, s32[2048]{0:T(1024)S(1)} %copy-done.5), kind=kCustom, calls=%fused_computation.5 | custom fusion | bytes 2105344 | tf_op jit(solution)/shard_map/gather | solution.py:103
  359.2 8.5 %all_to_all.16 = bf16[2,2048,256]{2,1,0:T(8,128)(2,1)S(1)} all-to-all(bf16[2,2048,256]{2,1,0:T(8,128)(2,1)S(1)} %pad_maximum_fusion), channel_id=1, replica_groups=mesh['space'=128,'mp'=2] {'mp'}, dimensions={0} | all-to-all | bytes 4194304 | tf_op jit(solution)/shard_map/all_to_all | solution.py:105
  368.6 1.1 copy-done.1
  371.3 7.3 %fusion.32 = bf16[2048,512]{1,0:T(8,128)(2,1)} fusion(bf16[1024,512]{1,0:T(8,128)(2,1)S(1)} %copy-done, bf16[512,1024]{1,0:T(8,128)(2,1)} %param.18, bf16[2048,512]{1,0:T(8,128)(2,1)S(1)} %get-tuple-element.60, f32[512]{0:T(512)S(1)} %copy-done.11, f32[2048]{0:T(1024)S(1)} %add_rsqrt_fusion, f32[2048]{0:T(1024)S(1)} %broadcast_multiply_fusion), kind=kOutput, calls=%fused_computation.51 | convolution fusion | flops 4320133120 | bytes 6309888 | tf_op jit(solution)/shard_map/dot_general | solution.py:112
  378.6 9.6 %reduce-scatter.5.cloned.1.call-done = bf16[1024,512]{1,0:T(8,128)(2,1)} async-done(((bf16[2048,512]{1,0:T(8,128)(2,1)}), bf16[1024,512]{1,0:T(8,128)(2,1)}) %reduce-scatter.5.cloned.1.call-update) | async-done | bytes 1048592 | tf_op jit(solution)/shard_map/reduce_scatter | solution.py:111
  388.2 2.5 add_convert_fusion
  390.7 17.9 %all-gather.2.cloned.1.call-done = bf16[2048,512]{1,0:T(8,128)(2,1)} async-done(((bf16[1024,512]{1,0:T(8,128)(2,1)}), bf16[2048,512]{1,0:T(8,128)(2,1)}) %all-gather.2.cloned.1.call-update) | async-done | bytes 2097168 | tf_op jit(solution)/shard_map/all_gather | solution.py:119
  408.6 3.0 copy.48
  (63 shorter events, 5.7 us)
Async XLA Ops:
  6.5 364.7 %copy-start = (bf16[1024,512]{1,0:T(8,128)(2,1)S(1)}, bf16[1024,512]{1,0:T(8,128)(2,1)}, u32[]{:S(2)}) copy-start(bf16[1024,512]{1,0:T(8,128)(2,1)} %param.19) | copy-start | bytes 3145732
  6.5 4.5 %copy-start.7 = (s32[2048]{0:T(1024)S(1)}, s32[2048]{0:T(1024)}, u32[]{:S(2)}) copy-start(s32[2048]{0:T(1024)} %param.12) | copy-start | bytes 24580
  6.5 13.2 %copy-start.8 = (f32[512]{0:T(512)S(1)}, f32[512]{0:T(512)}, u32[]{:S(2)}) copy-start(f32[512]{0:T(512)} %param.14) | copy-start | bytes 6148
  31.1 16.7 %copy-start.9 = (s32[1,4]{1,0:T(1,128)S(1)}, s32[1,4]{1,0:T(1,128)}, u32[]{:S(2)}) copy-start(s32[1,4]{1,0:T(1,128)} %param.13) | copy-start | bytes 52
  31.1 65.8 %all-to-all-start = ((bf16[128,16,512]{2,1,0:T(8,128)(2,1)}), bf16[128,16,512]{2,1,0:T(8,128)(2,1)S(1)}, u32[]{:S(2)}, u32[]{:S(2)}) async-start(bf16[128,16,512]{2,1,0:T(8,128)(2,1)} %bitcast.79), calls=%async_computation | async-start | bytes 4194304 | tf_op jit(solution)/shard_map/all_to_all | solution.py:84
  47.5 261.6 %reduce-scatter.3.cloned.1.call-start = ((), (), s32[]{:S(2)}) async-start(), calls=%async_computation.5 | async-start | bytes 6291456 | tf_op jit(solution)/shard_map/reduce_scatter | solution.py:93
  96.9 1.4 copy-start.2
  98.2 2.5 copy-start.10
  98.2 2.6 copy-start.3
  103.2 178.8 %copy-start.6 = (s32[2048]{0:T(1024)S(1)}, s32[2048]{0:T(1024)}, u32[]{:S(2)}) copy-start(s32[2048]{0:T(1024)} %broadcast_clamp_fusion.1) | copy-start | bytes 24580
  282.0 8.6 %copy-start.4 = (bf16[256,512]{1,0:T(8,128)(2,1)S(1)}, bf16[256,512]{1,0:T(8,128)(2,1)}, u32[]{:S(2)}) copy-start(bf16[256,512]{1,0:T(8,128)(2,1)} %param.16) | copy-start | bytes 786436
  293.2 58.3 %copy-start.5 = (s32[2048]{0:T(1024)S(1)}, s32[2048]{0:T(1024)}, u32[]{:S(2)}) copy-start(s32[2048]{0:T(1024)} %get-tuple-element.61) | copy-start | bytes 24580
  293.2 95.0 %reduce-scatter.5.cloned.1.call-start = ((), (), s32[]{:S(2)}) async-start(), calls=%async_computation.6 | async-start | bytes 3145728 | tf_op jit(solution)/shard_map/reduce_scatter | solution.py:111
  368.0 1.6 copy-start.1
  369.6 1.6 copy-start.11
  378.5 30.1 %all-gather.2.cloned.1.call-start = ((), (), s32[]{:S(2)}) async-start(), calls=%async_computation.7 | async-start | bytes 3145728 | tf_op jit(solution)/shard_map/all_gather | solution.py:119
Sparse Core Ops, SparseCore 0:
  293.4 15.7 reduce-scatter.2
  378.7 9.4 reduce-scatter.4
  390.8 17.7 all-gather.1
